TPU v7x, 32 devices: a whole 2x2x4 slice. The times are simulated.
32 devices in a mesh: sweep: 4 (over x, core), bulk: 8 (over z, y).
Axes of the slice: x: 2, y: 2, z: 4, core: 2. Of those that a mesh axis runs over, the one named last changes fastest.
Arguments:
- source: float32 [128, 5, 128, 128], P('sweep', None, 'bulk'), may hold values from -6 to 6
- psi_old: float32 [128, 5, 128, 128], P('sweep', None, 'bulk'), may hold values from -6 to 6
- lateral: float32 [128, 2, 128, 128], P('sweep', None, 'bulk'), may hold values from 0.1 to 0.6
- lower_jac: float32 [128, 5, 5, 128, 128], P('sweep', None, None, 'bulk')
- upper_jac: float32 [128, 5, 5, 128, 128], P('sweep', None, None, 'bulk')
- diag_inv: float32 [128, 5, 5, 128, 128], P('sweep', None, None, 'bulk')
- face_weight: float32 [5, 65536], P(None, ('sweep', 'bulk')), may hold values from -6 to 6
- face_cell: int32 [65536], P(('sweep', 'bulk')), may hold values from 0 to 65535
- face_owner: int32 [65536, 1], P(('sweep', 'bulk')), may hold values from 0 to 7; in each aligned block of 2048 rows (0 to 2047, 2048 to 4095, ...) at most 512 rows name the same one
- face_node: int32 [65536], P(('sweep', 'bulk')), may hold values from 0 to 16383
- face_count: int32 [32], P(('sweep', 'bulk')), may hold values from 1 to 2048, as said below
Outputs:
- adjoint: float32 [128, 5, 128, 128], P('sweep', None, 'bulk')
- node_sens: float32 [131072], P('bulk')
Inputs may be any that keep to these rules, and one draw needn't show every extreme that they name: `face_owner`: among the 2048 faces of one device no owner appears more than 512 times; some device reaches 512. `face_count`: some device has all 2048 slots live.
All inputs are finite; a program needn't handle non-finite values.
Results may differ from a plain program's by a relative error of at most 0.00011.
Values sent between devices are 32-bit elements; how exact they have to be, the bound alone decides.
No kernel may reach another device: no remote copies, remote signals or barrier semaphores. Data moves between devices by JAX's collectives and lax.ppermute only.
A program may use at most 128 MiB of HBM per device.

v0:
```python
import jax
import jax.numpy as jnp
from jax import lax
from jax.sharding import PartitionSpec as P

NODES_DEV = 16384


def padded_2(value, sides, width):
    for axis, dim in sides:
        size, length = (lax.axis_size(axis), value.shape[dim])
        up = [(i, (i + 1) % size) for i in range(size - 1)]
        down = [(j, i) for i, j in up]
        last = lax.slice_in_dim(value, length - width, length, axis=dim)
        initial = lax.slice_in_dim(value, 0, width, axis=dim)
        before = lax.ppermute(last, axis, up)
        after = lax.ppermute(initial, axis, down)
        value = jnp.concatenate([before, value, after], axis=dim)
    return value


def from_behind(value, axis, by):
    length = lax.axis_size(axis)
    pairs = [(i, i + by) for i in range(length) if 0 <= i + by < length]
    return lax.ppermute(value, axis, pairs)


def matvec(matrix, vector):
    return jnp.sum(matrix * vector[None], axis=1)


def matmat(matrix, other):
    return jnp.sum(matrix[:, :, None] * other[None], axis=1)


def forward_sweep(right_side, lower_jac, diag_inv, start):

    def forward_advance(current, planes):
        rhs_plane, lower_plane, inv_plane = planes
        updated = matvec(inv_plane, rhs_plane - matvec(lower_plane, current))
        return (updated, updated)

    leaving, fields = lax.scan(
        forward_advance, start, (right_side, lower_jac, diag_inv), unroll=True
    )
    return fields


def backward_sweep(forward_field, upper_jac, diag_inv, start):

    def backward_advance(current, planes):
        fwd_plane, upper_plane, inv_plane = planes
        updated = fwd_plane - matvec(inv_plane, matvec(upper_plane, current))
        return (updated, updated)

    leaving, fields = lax.scan(
        backward_advance, start, (forward_field, upper_jac, diag_inv), reverse=True, unroll=True
    )
    return fields


def block_affine(given, coupled, diag_inv, identity, zero_state, backward):

    def block_advance(carry, planes):
        transfer, current = carry
        given_plane, coupled_plane, inv_plane = planes
        transfer = -matmat(inv_plane, matmat(coupled_plane, transfer))
        if backward:
            current = given_plane - matvec(inv_plane, matvec(coupled_plane, current))
        else:
            current = matvec(inv_plane, given_plane - matvec(coupled_plane, current))
        return ((transfer, current), 0)

    result, unused = lax.scan(
        block_advance,
        (identity, zero_state),
        (given, coupled, diag_inv),
        reverse=backward,
        unroll=True,
    )
    return result


def per_device(
    source,
    psi_old,
    lateral,
    lower_jac,
    upper_jac,
    diag_inv,
    face_weight,
    face_cell,
    face_owner,
    face_node,
    face_count,
):
    padded = padded_2(psi_old, (("bulk", 2),), 1)
    right_side = source - lateral[:, 0:1] * padded[:, :, :-2] - lateral[:, 1:2] * padded[:, :, 2:]
    zero_state = jnp.zeros(source.shape[1:], jnp.float32)
    identity = jnp.broadcast_to(
        jnp.eye(5, dtype=jnp.float32)[:, :, None, None], (5, 5) + source.shape[2:]
    )
    transfer, leaving = block_affine(right_side, lower_jac, diag_inv, identity, zero_state, False)
    boundary = zero_state
    for relay_step in range(lax.axis_size("sweep") - 1):
        boundary = from_behind(matvec(transfer, boundary) + leaving, "sweep", 1)
    forward_field = forward_sweep(right_side, lower_jac, diag_inv, boundary)
    transfer, leaving = block_affine(forward_field, upper_jac, diag_inv, identity, zero_state, True)
    boundary = zero_state
    for relay_step in range(lax.axis_size("sweep") - 1):
        boundary = from_behind(matvec(transfer, boundary) + leaving, "sweep", -1)
    adjoint = backward_sweep(forward_field, upper_jac, diag_inv, boundary)
    width_j = source.shape[2]
    width_k = source.shape[3]
    slots = face_cell.shape[0]
    plane_index = face_cell // (width_j * width_k)
    rest_index = face_cell % (width_j * width_k)
    column_index = rest_index // width_k
    depth_index = rest_index % width_k
    at_faces = adjoint[plane_index, :, column_index, depth_index]
    partial_value = jnp.sum(at_faces * face_weight.T, axis=1)
    active = jnp.arange(slots, dtype=jnp.int32) < face_count[0]
    partial_value = jnp.where(active, partial_value, jnp.float32(0.0))
    owner_dev = face_owner[:, 0]
    owners = lax.axis_size("bulk")
    dense_sums = jax.ops.segment_sum(
        partial_value, owner_dev * NODES_DEV + face_node, num_segments=NODES_DEV * owners
    )
    summed = lax.psum(dense_sums, ("sweep", "bulk"))
    node_sens = lax.dynamic_slice_in_dim(summed, lax.axis_index("bulk") * NODES_DEV, NODES_DEV)
    return (adjoint, node_sens)


def solution(mesh):
    placed = (
        P("sweep", None, "bulk", None),
        P("sweep", None, "bulk", None),
        P("sweep", None, "bulk", None),
        P("sweep", None, None, "bulk", None),
        P("sweep", None, None, "bulk", None),
        P("sweep", None, None, "bulk", None),
        P(None, ("sweep", "bulk")),
        P(("sweep", "bulk")),
        P(("sweep", "bulk"), None),
        P(("sweep", "bulk")),
        P(("sweep", "bulk")),
    )
    return jax.shard_map(
        per_device,
        mesh=mesh,
        in_specs=placed,
        out_specs=(P("sweep", None, "bulk", None), P("bulk")),
        check_vma=False,
    )
```

profile of v0, /device:TPU:0, one launch (start us, length us, event | category | flops | bytes accessed | tf_op | source)
XLA Modules:
  0.0 318.8 jit_solution(10096926136467632355)
XLA Ops:
  7.2 1.6 fusion.88
  8.8 5.0 %collective-permute-start = (f32[32,5,1,128]{3,0,2,1:T(8,128)S(1)}, f32[32,5,1,128]{3,0,2,1:T(8,128)S(1)}, u32[]{:S(2)}, u32[]{:S(2)}) collective-permute-start(f32[32,5,1,128]{3,0,2,1:T(8,128)S(1)} %copy.123), channel_id=1, source_target_pairs={{0,1},{1,2},{2,3},{3,4},{4,5},{5,6},{6,7},{8,9},{9,10},{10,11},{11... | collective-permute-start | bytes 245768 | tf_op jit(solution)/shard_map/ppermute | solution.py:16
  13.8 1.3 collective-permute-start.1
  16.1 2.0 slice_bitcast_fusion.92
  18.1 2.1 slice_bitcast_fusion.32
  21.2 1.0 slice-done.1
  22.7 1.6 slice-done.4
  41.3 1.5 collective-permute-start.2
  43.6 4.2 %collective-permute-start.3 = (f32[5,16,128]{2,1,0:T(8,128)S(1)}, f32[5,16,128]{2,1,0:T(8,128)S(1)}, u32[]{:S(2)}, u32[]{:S(2)}) collective-permute-start(f32[5,16,128]{2,1,0:T(8,128)S(1)} %add.57), channel_id=1, source_target_pairs={{0,8},{8,16},{16,24},{1,9},{9,17},{17,25},{2,10},{10,18},{18,26},{... | collective-permute-start | bytes 122888 | tf_op jit(solution)/shard_map/ppermute | solution.py:25
  48.7 4.5 %collective-permute-start.4 = (f32[5,16,128]{2,1,0:T(8,128)S(1)}, f32[5,16,128]{2,1,0:T(8,128)S(1)}, u32[]{:S(2)}, u32[]{:S(2)}) collective-permute-start(f32[5,16,128]{2,1,0:T(8,128)S(1)} %add.58), channel_id=1, source_target_pairs={{0,8},{8,16},{16,24},{1,9},{9,17},{17,25},{2,10},{10,18},{18,26},{... | collective-permute-start | bytes 122888 | tf_op jit(solution)/shard_map/ppermute | solution.py:25
  58.9 1.4 collective-permute-start.5
  60.4 3.9 %collective-permute-done.5 = f32[5,16,128]{2,1,0:T(8,128)S(1)} collective-permute-done((f32[5,16,128]{2,1,0:T(8,128)S(1)}, f32[5,16,128]{2,1,0:T(8,128)S(1)}, u32[]{:S(2)}, u32[]{:S(2)}) %collective-permute-start.5) | collective-permute-done | bytes 40992 | tf_op jit(solution)/shard_map/ppermute | solution.py:25
  64.3 1.3 collective-permute-start.6
  65.6 4.6 %collective-permute-done.6 = f32[5,16,128]{2,1,0:T(8,128)S(1)} collective-permute-done((f32[5,16,128]{2,1,0:T(8,128)S(1)}, f32[5,16,128]{2,1,0:T(8,128)S(1)}, u32[]{:S(2)}, u32[]{:S(2)}) %collective-permute-start.6) | collective-permute-done | bytes 40992 | tf_op jit(solution)/shard_map/ppermute | solution.py:25
  70.8 1.5 collective-permute-start.7
  72.4 1.2 copy.122
  75.0 1.5 collective-permute-done.7
  76.5 1.0 multiply_reduce_fusion.191
  77.5 1.1 multiply_reduce_fusion.190
  78.6 1.0 sub.1037
  79.6 1.0 multiply_reduce_fusion.189
  80.6 1.0 multiply_reduce_fusion.188
  82.3 1.0 multiply_reduce_fusion.187
  83.3 1.0 multiply_reduce_fusion.186
  85.1 1.0 multiply_reduce_fusion.185
  86.0 1.0 multiply_reduce_fusion.184
  87.8 1.0 multiply_reduce_fusion.183
  88.7 1.0 multiply_reduce_fusion.182
  90.5 1.0 multiply_reduce_fusion.181
  91.5 1.0 multiply_reduce_fusion.180
  93.2 1.0 multiply_reduce_fusion.179
  94.2 1.0 multiply_reduce_fusion.178
  95.9 1.0 multiply_reduce_fusion.177
  96.9 1.0 multiply_reduce_fusion.176
  98.7 1.0 multiply_reduce_fusion.175
  99.6 1.0 multiply_reduce_fusion.174
  101.4 1.0 multiply_reduce_fusion.173
  102.3 1.0 multiply_reduce_fusion.172
  103.3 1.0 multiply_reduce_fusion.171
  104.3 1.0 multiply_reduce_fusion.170
  105.3 1.0 multiply_reduce_fusion.169
  106.3 1.0 multiply_reduce_fusion.167
  107.3 1.0 multiply_reduce_fusion.165
  108.3 1.0 multiply_reduce_fusion.163
  109.3 1.0 multiply_reduce_fusion.161
  110.4 1.0 multiply_reduce_fusion.159
  111.4 1.0 multiply_reduce_fusion.157
  112.4 1.0 multiply_reduce_fusion.155
  113.4 1.0 multiply_reduce_fusion.153
  114.4 1.0 multiply_reduce_fusion.151
  115.4 1.0 multiply_reduce_fusion.149
  116.4 1.0 multiply_reduce_fusion.147
  117.4 1.0 multiply_reduce_fusion.145
  119.4 1.0 multiply_reduce_fusion.141
  120.4 1.0 multiply_reduce_fusion.139
  121.5 1.0 multiply_reduce_fusion.137
  122.5 1.0 multiply_reduce_fusion.135
  123.5 1.0 multiply_reduce_fusion.133
  124.5 1.0 multiply_reduce_fusion.131
  126.9 16.5 %copy.121 = f32[32,5,16,128]{1,3,2,0:T(8,128)} copy(f32[32,5,16,128]{3,2,1,0:T(8,128)S(1)} %constant_dynamic-update-slice_fusion) | data formatting | bytes 2621440 | tf_op jit(solution)/shard_map/concatenate | solution.py:56
  143.4 22.2 %gather_fusion = f32[2048,5]{1,0:T(8,128)S(1)} fusion(f32[32,5,16,128]{1,3,2,0:T(8,128)} %copy.121, s32[2048]{0:T(1024)S(1)} %fusion.74), kind=kCustom, calls=%fused_computation | custom fusion | bytes 106496 | tf_op jit(solution)/shard_map/gather | solution.py:120
  166.0 12.2 %scatter_custom_fusion = f32[131072]{0:T(1024)} fusion(s32[2048]{0:T(1024)} %add.62, f32[2048]{0:T(1024)S(1)} %fusion.81, f32[]{:T(128)} %constant.53.clone.1), kind=kCustom, calls=%fused_computation.138 | custom fusion | flops 2048 | bytes 524800 | tf_op jit(solution)/shard_map/scatter-add | solution.py:126
  178.2 132.3 %all-reduce.2.cloned.1.call-done = f32[131072]{0:T(1024)} async-done(((f32[131072]{0:T(1024)}), f32[131072]{0:T(1024)}) %all-reduce.2.cloned.1.call-update) | async-done | bytes 524304 | tf_op jit(solution)/shard_map/psum | solution.py:129
  310.5 1.5 dynamic_slice.3
  (720 shorter events, 34.4 us)
Async XLA Ops:
  7.2 303.3 %all-reduce.2.cloned.1.call-start = ((), (), s32[]{:S(2)}) async-start(), calls=%async_computation | async-start | bytes 1048576 | tf_op jit(solution)/shard_map/psum | solution.py:129
  7.2 13.0 %copy-start = (f32[32,5,5,16,128]{4,3,2,1,0:T(8,128)S(1)}, f32[32,5,5,16,128]{4,3,2,1,0:T(8,128)}, u32[]{:S(2)}) copy-start(f32[32,5,5,16,128]{4,3,2,1,0:T(8,128)} %param.15) | copy-start | bytes 19660804
  8.8 29.5 %collective-permute-start = (f32[32,5,1,128]{3,0,2,1:T(8,128)S(1)}, f32[32,5,1,128]{3,0,2,1:T(8,128)S(1)}, u32[]{:S(2)}, u32[]{:S(2)}) collective-permute-start(f32[32,5,1,128]{3,0,2,1:T(8,128)S(1)} %copy.123), channel_id=1, source_target_pairs={{0,1},{1,2},{2,3},{3,4},{4,5},{5,6},{6,7},{8,9},{9,10},{10,11},{11... | collective-permute-start | bytes 245768 | tf_op jit(solution)/shard_map/ppermute | solution.py:16
  13.8 24.5 %collective-permute-start.1 = (f32[32,5,1,128]{3,0,2,1:T(8,128)S(1)}, f32[32,5,1,128]{3,0,2,1:T(8,128)S(1)}, u32[]{:S(2)}, u32[]{:S(2)}) collective-permute-start(f32[32,5,1,128]{3,0,2,1:T(8,128)S(1)} %copy.124), channel_id=1, source_target_pairs={{1,0},{2,1},{3,2},{4,3},{5,4},{6,5},{7,6},{9,8},{10,9},{11,10},{12... | collective-permute-start | bytes 245768 | tf_op jit(solution)/shard_map/ppermute | solution.py:17
  18.1 3.1 slice-start
  20.3 1.9 slice-start.1
  22.2 2.2 slice-start.4
  22.4 2.8 slice-start.5
  22.4 3.1 copy-start.52
  36.5 2.0 copy-start.1
  36.5 2.0 copy-start.3
  41.3 2.3 collective-permute-start.2
  43.6 5.0 %collective-permute-start.3 = (f32[5,16,128]{2,1,0:T(8,128)S(1)}, f32[5,16,128]{2,1,0:T(8,128)S(1)}, u32[]{:S(2)}, u32[]{:S(2)}) collective-permute-start(f32[5,16,128]{2,1,0:T(8,128)S(1)} %add.57), channel_id=1, source_target_pairs={{0,8},{8,16},{16,24},{1,9},{9,17},{17,25},{2,10},{10,18},{18,26},{... | collective-permute-start | bytes 122888 | tf_op jit(solution)/shard_map/ppermute | solution.py:25
  48.7 5.3 %collective-permute-start.4 = (f32[5,16,128]{2,1,0:T(8,128)S(1)}, f32[5,16,128]{2,1,0:T(8,128)S(1)}, u32[]{:S(2)}, u32[]{:S(2)}) collective-permute-start(f32[5,16,128]{2,1,0:T(8,128)S(1)} %add.58), channel_id=1, source_target_pairs={{0,8},{8,16},{16,24},{1,9},{9,17},{17,25},{2,10},{10,18},{18,26},{... | collective-permute-start | bytes 122888 | tf_op jit(solution)/shard_map/ppermute | solution.py:25
  54.3 4.4 %copy-start.4 = (f32[5,16,128]{2,1,0:T(8,128)}, f32[5,16,128]{2,1,0:T(8,128)S(1)}, u32[]{:S(2)}) copy-start(f32[5,16,128]{2,1,0:T(8,128)S(1)} %multiply_reduce_fusion.315) | copy-start | bytes 122884
  54.4 4.2 %copy-start.6 = (f32[5,16,128]{2,1,0:T(8,128)}, f32[5,16,128]{2,1,0:T(8,128)S(1)}, u32[]{:S(2)}) copy-start(f32[5,16,128]{2,1,0:T(8,128)S(1)} %multiply_reduce_fusion.313) | copy-start | bytes 122884
  54.5 4.1 %copy-start.8 = (f32[5,16,128]{2,1,0:T(8,128)}, f32[5,16,128]{2,1,0:T(8,128)S(1)}, u32[]{:S(2)}) copy-start(f32[5,16,128]{2,1,0:T(8,128)S(1)} %multiply_reduce_fusion.311) | copy-start | bytes 122884
  54.5 3.9 %copy-start.10 = (f32[5,16,128]{2,1,0:T(8,128)}, f32[5,16,128]{2,1,0:T(8,128)S(1)}, u32[]{:S(2)}) copy-start(f32[5,16,128]{2,1,0:T(8,128)S(1)} %multiply_reduce_fusion.309) | copy-start | bytes 122884
  54.6 3.8 %copy-start.12 = (f32[5,16,128]{2,1,0:T(8,128)}, f32[5,16,128]{2,1,0:T(8,128)S(1)}, u32[]{:S(2)}) copy-start(f32[5,16,128]{2,1,0:T(8,128)S(1)} %multiply_reduce_fusion.307) | copy-start | bytes 122884
  54.7 3.6 %copy-start.14 = (f32[5,16,128]{2,1,0:T(8,128)}, f32[5,16,128]{2,1,0:T(8,128)S(1)}, u32[]{:S(2)}) copy-start(f32[5,16,128]{2,1,0:T(8,128)S(1)} %multiply_reduce_fusion.305) | copy-start | bytes 122884
  54.8 3.5 %copy-start.16 = (f32[5,16,128]{2,1,0:T(8,128)}, f32[5,16,128]{2,1,0:T(8,128)S(1)}, u32[]{:S(2)}) copy-start(f32[5,16,128]{2,1,0:T(8,128)S(1)} %multiply_reduce_fusion.303) | copy-start | bytes 122884
  54.9 3.3 %copy-start.18 = (f32[5,16,128]{2,1,0:T(8,128)}, f32[5,16,128]{2,1,0:T(8,128)S(1)}, u32[]{:S(2)}) copy-start(f32[5,16,128]{2,1,0:T(8,128)S(1)} %multiply_reduce_fusion.301) | copy-start | bytes 122884
  54.9 3.1 copy-start.20
  55.0 3.0 copy-start.22
  55.1 2.8 copy-start.24
  55.2 2.6 copy-start.26
  55.2 2.5 copy-start.28
  55.3 2.3 copy-start.30
  55.4 2.1 copy-start.32
  55.5 2.0 copy-start.34
  55.6 1.8 copy-start.36
  55.6 1.6 copy-start.38
  56.3 1.5 copy-start.50
  56.4 1.5 copy-start.51
  56.5 1.5 copy-start.53
  57.4 8.1 %copy-start.55 = (s32[2048,1]{0,1:T(1,128)S(1)}, s32[2048,1]{0,1:T(1,128)}, u32[]{:S(2)}) copy-start(s32[2048,1]{0,1:T(1,128)} %param.19) | copy-start | bytes 24580
  57.5 14.9 %copy-start.56 = (s32[2048]{0:T(1024)S(1)}, s32[2048]{0:T(1024)}, u32[]{:S(2)}) copy-start(s32[2048]{0:T(1024)} %param.18) | copy-start | bytes 24580
  57.7 16.8 %copy-start.54 = (s32[2048]{0:T(1024)S(1)}, s32[2048]{0:T(1024)}, u32[]{:S(2)}) copy-start(s32[2048]{0:T(1024)} %param.20) | copy-start | bytes 24580
  58.4 47.8 %slice-start.2 = ((s8[6553600]{0:T(1024)(128)(4,1)}), s8[2359296]{0:T(1024)(128)(4,1)S(1)}, s32[]{:S(2)}) async-start(s8[6553600]{0:T(1024)(128)(4,1)} %bitcast.1165), calls=%async_computation.3 | async-start | bytes 4718592
  58.9 5.3 %collective-permute-start.5 = (f32[5,16,128]{2,1,0:T(8,128)S(1)}, f32[5,16,128]{2,1,0:T(8,128)S(1)}, u32[]{:S(2)}, u32[]{:S(2)}) collective-permute-start(f32[5,16,128]{2,1,0:T(8,128)S(1)} %get-tuple-element.10), channel_id=1, source_target_pairs={{8,0},{16,8},{24,16},{9,1},{17,9},{25,17},{10,2},{18,10},{26,18},{... | collective-permute-start | bytes 122888 | tf_op jit(solution)/shard_map/ppermute | solution.py:25
  64.3 5.9 %collective-permute-start.6 = (f32[5,16,128]{2,1,0:T(8,128)S(1)}, f32[5,16,128]{2,1,0:T(8,128)S(1)}, u32[]{:S(2)}, u32[]{:S(2)}) collective-permute-start(f32[5,16,128]{2,1,0:T(8,128)S(1)} %add.60), channel_id=1, source_target_pairs={{8,0},{16,8},{24,16},{9,1},{17,9},{25,17},{10,2},{18,10},{26,18},{... | collective-permute-start | bytes 122888 | tf_op jit(solution)/shard_map/ppermute | solution.py:25
  70.8 5.7 %collective-permute-start.7 = (f32[5,16,128]{2,1,0:T(8,128)}, f32[5,16,128]{2,1,0:T(8,128)}, u32[]{:S(2)}, u32[]{:S(2)}) collective-permute-start(f32[5,16,128]{2,1,0:T(8,128)} %add.61), channel_id=1, source_target_pairs={{8,0},{16,8},{24,16},{9,1},{17,9},{25,17},{10,2},{18,10},{26,18},{... | collective-permute-start | bytes 122888 | tf_op jit(solution)/shard_map/ppermute | solution.py:25
  73.6 29.7 %copy-start.43 = (f32[5,16,128]{2,1,0:T(8,128)S(1)}, f32[5,16,128]{2,1,0:T(8,128)}, u32[]{:S(2)}) copy-start(f32[5,16,128]{2,1,0:T(8,128)} %copy-done.42) | copy-start | bytes 122884
  73.6 31.6 %copy-start.41 = (f32[5,16,128]{2,1,0:T(8,128)S(1)}, f32[5,16,128]{2,1,0:T(8,128)}, u32[]{:S(2)}) copy-start(f32[5,16,128]{2,1,0:T(8,128)} %copy-done.40) | copy-start | bytes 122884
  73.6 32.7 %copy-start.39 = (f32[5,16,128]{2,1,0:T(8,128)S(1)}, f32[5,16,128]{2,1,0:T(8,128)}, u32[]{:S(2)}) copy-start(f32[5,16,128]{2,1,0:T(8,128)} %copy-done.38) | copy-start | bytes 122884
  73.6 33.7 %copy-start.37 = (f32[5,16,128]{2,1,0:T(8,128)S(1)}, f32[5,16,128]{2,1,0:T(8,128)}, u32[]{:S(2)}) copy-start(f32[5,16,128]{2,1,0:T(8,128)} %copy-done.36) | copy-start | bytes 122884
  73.6 34.7 %copy-start.35 = (f32[5,16,128]{2,1,0:T(8,128)S(1)}, f32[5,16,128]{2,1,0:T(8,128)}, u32[]{:S(2)}) copy-start(f32[5,16,128]{2,1,0:T(8,128)} %copy-done.34) | copy-start | bytes 122884
  73.7 35.7 %copy-start.33 = (f32[5,16,128]{2,1,0:T(8,128)S(1)}, f32[5,16,128]{2,1,0:T(8,128)}, u32[]{:S(2)}) copy-start(f32[5,16,128]{2,1,0:T(8,128)} %copy-done.32) | copy-start | bytes 122884
  73.7 36.7 %copy-start.31 = (f32[5,16,128]{2,1,0:T(8,128)S(1)}, f32[5,16,128]{2,1,0:T(8,128)}, u32[]{:S(2)}) copy-start(f32[5,16,128]{2,1,0:T(8,128)} %copy-done.30) | copy-start | bytes 122884
  73.7 37.7 %copy-start.29 = (f32[5,16,128]{2,1,0:T(8,128)S(1)}, f32[5,16,128]{2,1,0:T(8,128)}, u32[]{:S(2)}) copy-start(f32[5,16,128]{2,1,0:T(8,128)} %copy-done.28) | copy-start | bytes 122884
  73.7 38.7 %copy-start.27 = (f32[5,16,128]{2,1,0:T(8,128)S(1)}, f32[5,16,128]{2,1,0:T(8,128)}, u32[]{:S(2)}) copy-start(f32[5,16,128]{2,1,0:T(8,128)} %copy-done.26) | copy-start | bytes 122884
  75.0 38.3 %copy-start.25 = (f32[5,16,128]{2,1,0:T(8,128)S(1)}, f32[5,16,128]{2,1,0:T(8,128)}, u32[]{:S(2)}) copy-start(f32[5,16,128]{2,1,0:T(8,128)} %copy-done.24) | copy-start | bytes 122884
  77.5 28.8 %slice-start.3 = ((s8[6553600]{0:T(1024)(128)(4,1)}), s8[4194304]{0:T(1024)(128)(4,1)S(1)}, s32[]{:S(2)}) async-start(s8[6553600]{0:T(1024)(128)(4,1)} %bitcast.1165), calls=%async_computation.4 | async-start | bytes 8388608
  79.6 34.7 %copy-start.23 = (f32[5,16,128]{2,1,0:T(8,128)S(1)}, f32[5,16,128]{2,1,0:T(8,128)}, u32[]{:S(2)}) copy-start(f32[5,16,128]{2,1,0:T(8,128)} %copy-done.22) | copy-start | bytes 122884
  82.3 33.0 %copy-start.21 = (f32[5,16,128]{2,1,0:T(8,128)S(1)}, f32[5,16,128]{2,1,0:T(8,128)}, u32[]{:S(2)}) copy-start(f32[5,16,128]{2,1,0:T(8,128)} %copy-done.20) | copy-start | bytes 122884
  85.1 31.3 %copy-start.19 = (f32[5,16,128]{2,1,0:T(8,128)S(1)}, f32[5,16,128]{2,1,0:T(8,128)}, u32[]{:S(2)}) copy-start(f32[5,16,128]{2,1,0:T(8,128)} %copy-done.18) | copy-start | bytes 122884
  87.8 29.6 %copy-start.17 = (f32[5,16,128]{2,1,0:T(8,128)S(1)}, f32[5,16,128]{2,1,0:T(8,128)}, u32[]{:S(2)}) copy-start(f32[5,16,128]{2,1,0:T(8,128)} %copy-done.16) | copy-start | bytes 122884
  90.5 27.9 %copy-start.15 = (f32[5,16,128]{2,1,0:T(8,128)S(1)}, f32[5,16,128]{2,1,0:T(8,128)}, u32[]{:S(2)}) copy-start(f32[5,16,128]{2,1,0:T(8,128)} %copy-done.14) | copy-start | bytes 122884
  93.2 26.2 %copy-start.13 = (f32[5,16,128]{2,1,0:T(8,128)S(1)}, f32[5,16,128]{2,1,0:T(8,128)}, u32[]{:S(2)}) copy-start(f32[5,16,128]{2,1,0:T(8,128)} %copy-done.12) | copy-start | bytes 122884
  95.9 24.5 %copy-start.11 = (f32[5,16,128]{2,1,0:T(8,128)S(1)}, f32[5,16,128]{2,1,0:T(8,128)}, u32[]{:S(2)}) copy-start(f32[5,16,128]{2,1,0:T(8,128)} %copy-done.10) | copy-start | bytes 122884
  98.7 22.8 %copy-start.9 = (f32[5,16,128]{2,1,0:T(8,128)S(1)}, f32[5,16,128]{2,1,0:T(8,128)}, u32[]{:S(2)}) copy-start(f32[5,16,128]{2,1,0:T(8,128)} %copy-done.8) | copy-start | bytes 122884
  101.4 21.1 %copy-start.7 = (f32[5,16,128]{2,1,0:T(8,128)S(1)}, f32[5,16,128]{2,1,0:T(8,128)}, u32[]{:S(2)}) copy-start(f32[5,16,128]{2,1,0:T(8,128)} %copy-done.6) | copy-start | bytes 122884
  103.3 20.1 %copy-start.5 = (f32[5,16,128]{2,1,0:T(8,128)S(1)}, f32[5,16,128]{2,1,0:T(8,128)}, u32[]{:S(2)}) copy-start(f32[5,16,128]{2,1,0:T(8,128)} %copy-done.4) | copy-start | bytes 122884
  126.9 16.5 %copy-start.2 = (f32[32,5,16,128]{3,2,1,0:T(8,128)}, f32[32,5,16,128]{3,2,1,0:T(8,128)S(1)}, u32[]{:S(2)}) copy-start(f32[32,5,16,128]{3,2,1,0:T(8,128)S(1)} %constant_dynamic-update-slice_fusion) | copy-start | bytes 3932164
  (8 other events, 11.5 us)
Sparse Core Ops, SparseCore 0:
  178.3 132.1 all-reduce.1
where the time goes:
time: 321 us; the launch traced here: 319 us
  waiting for transfers between devices  145 us (45%)
  other arithmetic  81.3 us (25%)
  local copies, waits for them, and re-layouts  52.9 us (16%)
  starting transfers between devices  20.7 us (6%)
  between operations  19.2 us (6%)
    psum x1, waiting for transfers between devices, per_device(): summed = lax.psum(dense_sums, ('sweep', 'bulk'))  132 us
    reduce_sum x260, other arithmetic, matvec(): return jnp.sum(matrix * vector[None], axis=1)  46.8 us
    gather x1, local copies, waits for them, and re-layouts, per_device(): at_faces = adjoint[plane_index, :, column_index, depth_index]  22.2 us
    concatenate x2, local copies, waits for them, and re-layouts, backward_sweep(): lax.scan(backward_advance, start, (forward_field, upper_jac, diag_inv), r...  16.5 us
    ppermute x6, starting transfers between devices, from_behind(): return lax.ppermute(value, axis, pairs)  14.3 us
    ppermute x6, waiting for transfers between devices, from_behind(): return lax.ppermute(value, axis, pairs)  12.4 us
    scatter-add x1, other arithmetic, per_device(): jax.ops.segment_sum(partial_value, owner_dev * NODES_DEV + face_node, num...  12.2 us
    reduce_sum x126, other arithmetic, matmat(): return jnp.sum(matrix[:, :, None] * other[None], axis=1)  10.7 us
  transfers between devices with their start and end apart: 9, of which 7 were waited for; matrix products, arithmetic and copies ran while one was open for 6% of the time, Pallas kernels for 0%

commit v1 on v0

--- a/solution.py
+++ b/solution.py
@@ -126,7 +126,7 @@
     dense_sums = jax.ops.segment_sum(
         partial_value, owner_dev * NODES_DEV + face_node, num_segments=NODES_DEV * owners
     )
-    summed = lax.psum(dense_sums, ("sweep", "bulk"))
+    summed = lax.psum(lax.psum(dense_sums, "bulk"), "sweep")
     node_sens = lax.dynamic_slice_in_dim(summed, lax.axis_index("bulk") * NODES_DEV, NODES_DEV)
     return (adjoint, node_sens)
 

time: 321 us -> 300 us (0.935)
  waiting for transfers between devices: 145 us -> 124 us
    psum x1 -> x2, waiting for transfers between devices: 132 us -> 112 us  [per_device(): summed = lax.psum(lax.psum(dense_sums, 'bulk'), 'sweep')]
  transfers between devices with their start and end apart: 9 -> 10, of which waited for: 7 -> 8; matrix products, arithmetic and copies ran while one was open for 6% -> 7% of each run, Pallas kernels for 0% -> 0%
where the time goes in v1:
time: 300 us; the launch traced here: 298 us
  waiting for transfers between devices  124 us (41%)
  other arithmetic  81.4 us (27%)
  local copies, waits for them, and re-layouts  52.9 us (18%)
  starting transfers between devices  20.7 us (7%)
  between operations  19.2 us (6%)
    psum x2, waiting for transfers between devices, per_device(): summed = lax.psum(lax.psum(dense_sums, 'bulk'), 'sweep')  112 us
    reduce_sum x260, other arithmetic, matvec(): return jnp.sum(matrix * vector[None], axis=1)  46.8 us
    gather x1, local copies, waits for them, and re-layouts, per_device(): at_faces = adjoint[plane_index, :, column_index, depth_index]  22.2 us
    concatenate x2, local copies, waits for them, and re-layouts, backward_sweep(): lax.scan(backward_advance, start, (forward_field, upper_jac, diag_inv), r...  16.5 us
    ppermute x6, starting transfers between devices, from_behind(): return lax.ppermute(value, axis, pairs)  14.3 us
    ppermute x6, waiting for transfers between devices, from_behind(): return lax.ppermute(value, axis, pairs)  12.4 us
    scatter-add x1, other arithmetic, per_device(): jax.ops.segment_sum(partial_value, owner_dev * NODES_DEV + face_node, num...  12.2 us
    reduce_sum x126, other arithmetic, matmat(): return jnp.sum(matrix[:, :, None] * other[None], axis=1)  10.7 us
  transfers between devices with their start and end apart: 10, of which 8 were waited for; matrix products, arithmetic and copies ran while one was open for 7% of the time, Pallas kernels for 0%

profile of v1, /device:TPU:0, one launch (start us, length us, event | category | flops | bytes accessed | tf_op | source)
XLA Modules:
  0.0 298.3 jit_solution(6646469095780531807)
XLA Ops:
  7.2 1.6 fusion.88
  8.8 5.0 %collective-permute-start = (f32[32,5,1,128]{3,0,2,1:T(8,128)S(1)}, f32[32,5,1,128]{3,0,2,1:T(8,128)S(1)}, u32[]{:S(2)}, u32[]{:S(2)}) collective-permute-start(f32[32,5,1,128]{3,0,2,1:T(8,128)S(1)} %copy.123), channel_id=1, source_target_pairs={{0,1},{1,2},{2,3},{3,4},{4,5},{5,6},{6,7},{8,9},{9,10},{10,11},{11... | collective-permute-start | bytes 245768 | tf_op jit(solution)/shard_map/ppermute | solution.py:16
  13.8 1.3 collective-permute-start.1
  16.1 2.0 slice_bitcast_fusion.92
  18.1 2.1 slice_bitcast_fusion.32
  21.2 1.0 slice-done.1
  22.7 1.6 slice-done.4
  41.3 1.5 collective-permute-start.2
  43.6 4.2 %collective-permute-start.3 = (f32[5,16,128]{2,1,0:T(8,128)S(1)}, f32[5,16,128]{2,1,0:T(8,128)S(1)}, u32[]{:S(2)}, u32[]{:S(2)}) collective-permute-start(f32[5,16,128]{2,1,0:T(8,128)S(1)} %add.59), channel_id=1, source_target_pairs={{0,8},{8,16},{16,24},{1,9},{9,17},{17,25},{2,10},{10,18},{18,26},{... | collective-permute-start | bytes 122888 | tf_op jit(solution)/shard_map/ppermute | solution.py:25
  48.7 4.5 %collective-permute-start.4 = (f32[5,16,128]{2,1,0:T(8,128)S(1)}, f32[5,16,128]{2,1,0:T(8,128)S(1)}, u32[]{:S(2)}, u32[]{:S(2)}) collective-permute-start(f32[5,16,128]{2,1,0:T(8,128)S(1)} %add.60), channel_id=1, source_target_pairs={{0,8},{8,16},{16,24},{1,9},{9,17},{17,25},{2,10},{10,18},{18,26},{... | collective-permute-start | bytes 122888 | tf_op jit(solution)/shard_map/ppermute | solution.py:25
  58.9 1.4 collective-permute-start.5
  60.4 3.9 %collective-permute-done.5 = f32[5,16,128]{2,1,0:T(8,128)S(1)} collective-permute-done((f32[5,16,128]{2,1,0:T(8,128)S(1)}, f32[5,16,128]{2,1,0:T(8,128)S(1)}, u32[]{:S(2)}, u32[]{:S(2)}) %collective-permute-start.5) | collective-permute-done | bytes 40992 | tf_op jit(solution)/shard_map/ppermute | solution.py:25
  64.3 1.3 collective-permute-start.6
  65.6 4.6 %collective-permute-done.6 = f32[5,16,128]{2,1,0:T(8,128)S(1)} collective-permute-done((f32[5,16,128]{2,1,0:T(8,128)S(1)}, f32[5,16,128]{2,1,0:T(8,128)S(1)}, u32[]{:S(2)}, u32[]{:S(2)}) %collective-permute-start.6) | collective-permute-done | bytes 40992 | tf_op jit(solution)/shard_map/ppermute | solution.py:25
  70.8 1.5 collective-permute-start.7
  72.4 1.2 copy.122
  75.0 1.5 collective-permute-done.7
  76.5 1.0 multiply_reduce_fusion.191
  77.5 1.1 multiply_reduce_fusion.190
  78.6 1.0 sub.1037
  79.6 1.0 multiply_reduce_fusion.189
  80.6 1.0 multiply_reduce_fusion.188
  82.3 1.0 multiply_reduce_fusion.187
  83.3 1.0 multiply_reduce_fusion.186
  85.1 1.0 multiply_reduce_fusion.185
  86.0 1.0 multiply_reduce_fusion.184
  87.8 1.0 multiply_reduce_fusion.183
  88.7 1.0 multiply_reduce_fusion.182
  90.5 1.0 multiply_reduce_fusion.181
  91.5 1.0 multiply_reduce_fusion.180
  93.2 1.0 multiply_reduce_fusion.179
  94.2 1.0 multiply_reduce_fusion.178
  95.9 1.0 multiply_reduce_fusion.177
  96.9 1.0 multiply_reduce_fusion.176
  98.7 1.0 multiply_reduce_fusion.175
  99.6 1.0 multiply_reduce_fusion.174
  101.4 1.0 multiply_reduce_fusion.173
  102.3 1.0 multiply_reduce_fusion.172
  103.3 1.0 multiply_reduce_fusion.171
  104.3 1.0 multiply_reduce_fusion.170
  105.3 1.0 multiply_reduce_fusion.169
  106.3 1.0 multiply_reduce_fusion.167
  107.3 1.0 multiply_reduce_fusion.165
  108.3 1.0 multiply_reduce_fusion.163
  109.3 1.0 multiply_reduce_fusion.161
  110.4 1.0 multiply_reduce_fusion.159
  111.4 1.0 multiply_reduce_fusion.157
  112.4 1.0 multiply_reduce_fusion.155
  113.4 1.0 multiply_reduce_fusion.153
  114.4 1.0 multiply_reduce_fusion.151
  115.4 1.0 multiply_reduce_fusion.149
  117.4 1.0 multiply_reduce_fusion.145
  119.4 1.0 multiply_reduce_fusion.141
  120.4 1.0 multiply_reduce_fusion.139
  121.5 1.0 multiply_reduce_fusion.137
  122.5 1.0 multiply_reduce_fusion.135
  123.5 1.0 multiply_reduce_fusion.133
  124.5 1.0 multiply_reduce_fusion.131
  126.9 16.5 %copy.121 = f32[32,5,16,128]{1,3,2,0:T(8,128)} copy(f32[32,5,16,128]{3,2,1,0:T(8,128)S(1)} %constant_dynamic-update-slice_fusion) | data formatting | bytes 2621440 | tf_op jit(solution)/shard_map/concatenate | solution.py:56
  143.4 22.2 %gather_fusion = f32[2048,5]{1,0:T(8,128)S(1)} fusion(f32[32,5,16,128]{1,3,2,0:T(8,128)} %copy.121, s32[2048]{0:T(1024)S(1)} %fusion.74), kind=kCustom, calls=%fused_computation | custom fusion | bytes 106496 | tf_op jit(solution)/shard_map/gather | solution.py:120
  166.0 12.2 %scatter_custom_fusion = f32[131072]{0:T(1024)} fusion(s32[2048]{0:T(1024)} %add.64, f32[2048]{0:T(1024)S(1)} %fusion.81, f32[]{:T(128)} %constant.53.clone.1), kind=kCustom, calls=%fused_computation.138 | custom fusion | flops 2048 | bytes 524800 | tf_op jit(solution)/shard_map/scatter-add | solution.py:126
  178.2 76.8 %all-reduce.3.cloned.1.call-done = f32[131072]{0:T(1024)} async-done(((f32[131072]{0:T(1024)}), f32[131072]{0:T(1024)}) %all-reduce.3.cloned.1.call-update) | async-done | bytes 524304 | tf_op jit(solution)/shard_map/psum | solution.py:129
  255.0 34.9 %all-reduce.5.cloned.1.call-done = f32[131072]{0:T(1024)} async-done(((f32[131072]{0:T(1024)}), f32[131072]{0:T(1024)}) %all-reduce.5.cloned.1.call-update) | async-done | bytes 524304 | tf_op jit(solution)/shard_map/psum | solution.py:129
  290.0 1.5 dynamic_slice.3
  (723 shorter events, 35.5 us)
Async XLA Ops:
  7.2 247.8 %all-reduce.3.cloned.1.call-start = ((), (), s32[]{:S(2)}) async-start(), calls=%async_computation | async-start | bytes 1048576 | tf_op jit(solution)/shard_map/psum | solution.py:129
  7.2 13.0 %copy-start = (f32[32,5,5,16,128]{4,3,2,1,0:T(8,128)S(1)}, f32[32,5,5,16,128]{4,3,2,1,0:T(8,128)}, u32[]{:S(2)}) copy-start(f32[32,5,5,16,128]{4,3,2,1,0:T(8,128)} %param.15) | copy-start | bytes 19660804
  8.8 29.5 %collective-permute-start = (f32[32,5,1,128]{3,0,2,1:T(8,128)S(1)}, f32[32,5,1,128]{3,0,2,1:T(8,128)S(1)}, u32[]{:S(2)}, u32[]{:S(2)}) collective-permute-start(f32[32,5,1,128]{3,0,2,1:T(8,128)S(1)} %copy.123), channel_id=1, source_target_pairs={{0,1},{1,2},{2,3},{3,4},{4,5},{5,6},{6,7},{8,9},{9,10},{10,11},{11... | collective-permute-start | bytes 245768 | tf_op jit(solution)/shard_map/ppermute | solution.py:16
  13.8 24.5 %collective-permute-start.1 = (f32[32,5,1,128]{3,0,2,1:T(8,128)S(1)}, f32[32,5,1,128]{3,0,2,1:T(8,128)S(1)}, u32[]{:S(2)}, u32[]{:S(2)}) collective-permute-start(f32[32,5,1,128]{3,0,2,1:T(8,128)S(1)} %copy.124), channel_id=1, source_target_pairs={{1,0},{2,1},{3,2},{4,3},{5,4},{6,5},{7,6},{9,8},{10,9},{11,10},{12... | collective-permute-start | bytes 245768 | tf_op jit(solution)/shard_map/ppermute | solution.py:17
  18.1 3.1 %slice-start = ((s8[6553600]{0:T(1024)(128)(4,1)}), s8[4194304]{0:T(1024)(128)(4,1)S(1)}, s32[]{:S(2)}) async-start(s8[6553600]{0:T(1024)(128)(4,1)} %bitcast.1163), calls=%async_computation.2 | async-start | bytes 8388608
  20.3 1.9 slice-start.1
  22.2 2.2 slice-start.4
  22.4 2.8 slice-start.5
  22.4 3.1 %copy-start.52 = (f32[32,2,16,128]{3,2,1,0:T(8,128)S(1)}, f32[32,2,16,128]{3,2,1,0:T(8,128)}, u32[]{:S(2)}) copy-start(f32[32,2,16,128]{3,2,1,0:T(8,128)} %param.13) | copy-start | bytes 1572868
  36.5 2.0 copy-start.1
  36.5 2.0 copy-start.3
  41.3 2.3 collective-permute-start.2
  43.6 5.0 %collective-permute-start.3 = (f32[5,16,128]{2,1,0:T(8,128)S(1)}, f32[5,16,128]{2,1,0:T(8,128)S(1)}, u32[]{:S(2)}, u32[]{:S(2)}) collective-permute-start(f32[5,16,128]{2,1,0:T(8,128)S(1)} %add.59), channel_id=1, source_target_pairs={{0,8},{8,16},{16,24},{1,9},{9,17},{17,25},{2,10},{10,18},{18,26},{... | collective-permute-start | bytes 122888 | tf_op jit(solution)/shard_map/ppermute | solution.py:25
  48.7 5.3 %collective-permute-start.4 = (f32[5,16,128]{2,1,0:T(8,128)S(1)}, f32[5,16,128]{2,1,0:T(8,128)S(1)}, u32[]{:S(2)}, u32[]{:S(2)}) collective-permute-start(f32[5,16,128]{2,1,0:T(8,128)S(1)} %add.60), channel_id=1, source_target_pairs={{0,8},{8,16},{16,24},{1,9},{9,17},{17,25},{2,10},{10,18},{18,26},{... | collective-permute-start | bytes 122888 | tf_op jit(solution)/shard_map/ppermute | solution.py:25
  54.3 4.4 %copy-start.4 = (f32[5,16,128]{2,1,0:T(8,128)}, f32[5,16,128]{2,1,0:T(8,128)S(1)}, u32[]{:S(2)}) copy-start(f32[5,16,128]{2,1,0:T(8,128)S(1)} %multiply_reduce_fusion.315) | copy-start | bytes 122884
  54.4 4.2 %copy-start.6 = (f32[5,16,128]{2,1,0:T(8,128)}, f32[5,16,128]{2,1,0:T(8,128)S(1)}, u32[]{:S(2)}) copy-start(f32[5,16,128]{2,1,0:T(8,128)S(1)} %multiply_reduce_fusion.313) | copy-start | bytes 122884
  54.5 4.1 %copy-start.8 = (f32[5,16,128]{2,1,0:T(8,128)}, f32[5,16,128]{2,1,0:T(8,128)S(1)}, u32[]{:S(2)}) copy-start(f32[5,16,128]{2,1,0:T(8,128)S(1)} %multiply_reduce_fusion.311) | copy-start | bytes 122884
  54.5 3.9 %copy-start.10 = (f32[5,16,128]{2,1,0:T(8,128)}, f32[5,16,128]{2,1,0:T(8,128)S(1)}, u32[]{:S(2)}) copy-start(f32[5,16,128]{2,1,0:T(8,128)S(1)} %multiply_reduce_fusion.309) | copy-start | bytes 122884
  54.6 3.8 %copy-start.12 = (f32[5,16,128]{2,1,0:T(8,128)}, f32[5,16,128]{2,1,0:T(8,128)S(1)}, u32[]{:S(2)}) copy-start(f32[5,16,128]{2,1,0:T(8,128)S(1)} %multiply_reduce_fusion.307) | copy-start | bytes 122884
  54.7 3.6 %copy-start.14 = (f32[5,16,128]{2,1,0:T(8,128)}, f32[5,16,128]{2,1,0:T(8,128)S(1)}, u32[]{:S(2)}) copy-start(f32[5,16,128]{2,1,0:T(8,128)S(1)} %multiply_reduce_fusion.305) | copy-start | bytes 122884
  54.8 3.5 %copy-start.16 = (f32[5,16,128]{2,1,0:T(8,128)}, f32[5,16,128]{2,1,0:T(8,128)S(1)}, u32[]{:S(2)}) copy-start(f32[5,16,128]{2,1,0:T(8,128)S(1)} %multiply_reduce_fusion.303) | copy-start | bytes 122884
  54.9 3.3 %copy-start.18 = (f32[5,16,128]{2,1,0:T(8,128)}, f32[5,16,128]{2,1,0:T(8,128)S(1)}, u32[]{:S(2)}) copy-start(f32[5,16,128]{2,1,0:T(8,128)S(1)} %multiply_reduce_fusion.301) | copy-start | bytes 122884
  54.9 3.1 %copy-start.20 = (f32[5,16,128]{2,1,0:T(8,128)}, f32[5,16,128]{2,1,0:T(8,128)S(1)}, u32[]{:S(2)}) copy-start(f32[5,16,128]{2,1,0:T(8,128)S(1)} %multiply_reduce_fusion.299) | copy-start | bytes 122884
  55.0 3.0 copy-start.22
  55.1 2.8 copy-start.24
  55.2 2.6 copy-start.26
  55.2 2.5 copy-start.28
  55.3 2.3 copy-start.30
  55.4 2.1 copy-start.32
  55.5 2.0 copy-start.34
  55.6 1.8 copy-start.36
  55.6 1.6 copy-start.38
  56.4 1.5 copy-start.51
  56.5 1.5 copy-start.53
  57.4 8.1 %copy-start.55 = (s32[2048,1]{0,1:T(1,128)S(1)}, s32[2048,1]{0,1:T(1,128)}, u32[]{:S(2)}) copy-start(s32[2048,1]{0,1:T(1,128)} %param.19) | copy-start | bytes 24580
  57.5 14.9 %copy-start.56 = (s32[2048]{0:T(1024)S(1)}, s32[2048]{0:T(1024)}, u32[]{:S(2)}) copy-start(s32[2048]{0:T(1024)} %param.18) | copy-start | bytes 24580
  57.7 16.8 %copy-start.54 = (s32[2048]{0:T(1024)S(1)}, s32[2048]{0:T(1024)}, u32[]{:S(2)}) copy-start(s32[2048]{0:T(1024)} %param.20) | copy-start | bytes 24580
  58.4 47.8 %slice-start.2 = ((s8[6553600]{0:T(1024)(128)(4,1)}), s8[2359296]{0:T(1024)(128)(4,1)S(1)}, s32[]{:S(2)}) async-start(s8[6553600]{0:T(1024)(128)(4,1)} %bitcast.1165), calls=%async_computation.4 | async-start | bytes 4718592
  58.9 5.3 %collective-permute-start.5 = (f32[5,16,128]{2,1,0:T(8,128)S(1)}, f32[5,16,128]{2,1,0:T(8,128)S(1)}, u32[]{:S(2)}, u32[]{:S(2)}) collective-permute-start(f32[5,16,128]{2,1,0:T(8,128)S(1)} %get-tuple-element.10), channel_id=1, source_target_pairs={{8,0},{16,8},{24,16},{9,1},{17,9},{25,17},{10,2},{18,10},{26,18},{... | collective-permute-start | bytes 122888 | tf_op jit(solution)/shard_map/ppermute | solution.py:25
  64.3 5.9 %collective-permute-start.6 = (f32[5,16,128]{2,1,0:T(8,128)S(1)}, f32[5,16,128]{2,1,0:T(8,128)S(1)}, u32[]{:S(2)}, u32[]{:S(2)}) collective-permute-start(f32[5,16,128]{2,1,0:T(8,128)S(1)} %add.62), channel_id=1, source_target_pairs={{8,0},{16,8},{24,16},{9,1},{17,9},{25,17},{10,2},{18,10},{26,18},{... | collective-permute-start | bytes 122888 | tf_op jit(solution)/shard_map/ppermute | solution.py:25
  70.8 5.7 %collective-permute-start.7 = (f32[5,16,128]{2,1,0:T(8,128)}, f32[5,16,128]{2,1,0:T(8,128)}, u32[]{:S(2)}, u32[]{:S(2)}) collective-permute-start(f32[5,16,128]{2,1,0:T(8,128)} %add.63), channel_id=1, source_target_pairs={{8,0},{16,8},{24,16},{9,1},{17,9},{25,17},{10,2},{18,10},{26,18},{... | collective-permute-start | bytes 122888 | tf_op jit(solution)/shard_map/ppermute | solution.py:25
  73.6 29.7 %copy-start.43 = (f32[5,16,128]{2,1,0:T(8,128)S(1)}, f32[5,16,128]{2,1,0:T(8,128)}, u32[]{:S(2)}) copy-start(f32[5,16,128]{2,1,0:T(8,128)} %copy-done.42) | copy-start | bytes 122884
  73.6 31.6 %copy-start.41 = (f32[5,16,128]{2,1,0:T(8,128)S(1)}, f32[5,16,128]{2,1,0:T(8,128)}, u32[]{:S(2)}) copy-start(f32[5,16,128]{2,1,0:T(8,128)} %copy-done.40) | copy-start | bytes 122884
  73.6 32.7 %copy-start.39 = (f32[5,16,128]{2,1,0:T(8,128)S(1)}, f32[5,16,128]{2,1,0:T(8,128)}, u32[]{:S(2)}) copy-start(f32[5,16,128]{2,1,0:T(8,128)} %copy-done.38) | copy-start | bytes 122884
  73.6 33.7 %copy-start.37 = (f32[5,16,128]{2,1,0:T(8,128)S(1)}, f32[5,16,128]{2,1,0:T(8,128)}, u32[]{:S(2)}) copy-start(f32[5,16,128]{2,1,0:T(8,128)} %copy-done.36) | copy-start | bytes 122884
  73.6 34.7 %copy-start.35 = (f32[5,16,128]{2,1,0:T(8,128)S(1)}, f32[5,16,128]{2,1,0:T(8,128)}, u32[]{:S(2)}) copy-start(f32[5,16,128]{2,1,0:T(8,128)} %copy-done.34) | copy-start | bytes 122884
  73.7 35.7 %copy-start.33 = (f32[5,16,128]{2,1,0:T(8,128)S(1)}, f32[5,16,128]{2,1,0:T(8,128)}, u32[]{:S(2)}) copy-start(f32[5,16,128]{2,1,0:T(8,128)} %copy-done.32) | copy-start | bytes 122884
  73.7 36.7 %copy-start.31 = (f32[5,16,128]{2,1,0:T(8,128)S(1)}, f32[5,16,128]{2,1,0:T(8,128)}, u32[]{:S(2)}) copy-start(f32[5,16,128]{2,1,0:T(8,128)} %copy-done.30) | copy-start | bytes 122884
  73.7 37.7 %copy-start.29 = (f32[5,16,128]{2,1,0:T(8,128)S(1)}, f32[5,16,128]{2,1,0:T(8,128)}, u32[]{:S(2)}) copy-start(f32[5,16,128]{2,1,0:T(8,128)} %copy-done.28) | copy-start | bytes 122884
  73.7 38.7 %copy-start.27 = (f32[5,16,128]{2,1,0:T(8,128)S(1)}, f32[5,16,128]{2,1,0:T(8,128)}, u32[]{:S(2)}) copy-start(f32[5,16,128]{2,1,0:T(8,128)} %copy-done.26) | copy-start | bytes 122884
  75.0 38.3 %copy-start.25 = (f32[5,16,128]{2,1,0:T(8,128)S(1)}, f32[5,16,128]{2,1,0:T(8,128)}, u32[]{:S(2)}) copy-start(f32[5,16,128]{2,1,0:T(8,128)} %copy-done.24) | copy-start | bytes 122884
  77.5 28.8 %slice-start.3 = ((s8[6553600]{0:T(1024)(128)(4,1)}), s8[4194304]{0:T(1024)(128)(4,1)S(1)}, s32[]{:S(2)}) async-start(s8[6553600]{0:T(1024)(128)(4,1)} %bitcast.1165), calls=%async_computation.5 | async-start | bytes 8388608
  79.6 34.7 %copy-start.23 = (f32[5,16,128]{2,1,0:T(8,128)S(1)}, f32[5,16,128]{2,1,0:T(8,128)}, u32[]{:S(2)}) copy-start(f32[5,16,128]{2,1,0:T(8,128)} %copy-done.22) | copy-start | bytes 122884
  82.3 33.0 %copy-start.21 = (f32[5,16,128]{2,1,0:T(8,128)S(1)}, f32[5,16,128]{2,1,0:T(8,128)}, u32[]{:S(2)}) copy-start(f32[5,16,128]{2,1,0:T(8,128)} %copy-done.20) | copy-start | bytes 122884
  85.1 31.3 %copy-start.19 = (f32[5,16,128]{2,1,0:T(8,128)S(1)}, f32[5,16,128]{2,1,0:T(8,128)}, u32[]{:S(2)}) copy-start(f32[5,16,128]{2,1,0:T(8,128)} %copy-done.18) | copy-start | bytes 122884
  87.8 29.6 %copy-start.17 = (f32[5,16,128]{2,1,0:T(8,128)S(1)}, f32[5,16,128]{2,1,0:T(8,128)}, u32[]{:S(2)}) copy-start(f32[5,16,128]{2,1,0:T(8,128)} %copy-done.16) | copy-start | bytes 122884
  90.5 27.9 %copy-start.15 = (f32[5,16,128]{2,1,0:T(8,128)S(1)}, f32[5,16,128]{2,1,0:T(8,128)}, u32[]{:S(2)}) copy-start(f32[5,16,128]{2,1,0:T(8,128)} %copy-done.14) | copy-start | bytes 122884
  93.2 26.2 %copy-start.13 = (f32[5,16,128]{2,1,0:T(8,128)S(1)}, f32[5,16,128]{2,1,0:T(8,128)}, u32[]{:S(2)}) copy-start(f32[5,16,128]{2,1,0:T(8,128)} %copy-done.12) | copy-start | bytes 122884
  95.9 24.5 %copy-start.11 = (f32[5,16,128]{2,1,0:T(8,128)S(1)}, f32[5,16,128]{2,1,0:T(8,128)}, u32[]{:S(2)}) copy-start(f32[5,16,128]{2,1,0:T(8,128)} %copy-done.10) | copy-start | bytes 122884
  98.7 22.8 %copy-start.9 = (f32[5,16,128]{2,1,0:T(8,128)S(1)}, f32[5,16,128]{2,1,0:T(8,128)}, u32[]{:S(2)}) copy-start(f32[5,16,128]{2,1,0:T(8,128)} %copy-done.8) | copy-start | bytes 122884
  101.4 21.1 %copy-start.7 = (f32[5,16,128]{2,1,0:T(8,128)S(1)}, f32[5,16,128]{2,1,0:T(8,128)}, u32[]{:S(2)}) copy-start(f32[5,16,128]{2,1,0:T(8,128)} %copy-done.6) | copy-start | bytes 122884
  103.3 20.1 %copy-start.5 = (f32[5,16,128]{2,1,0:T(8,128)S(1)}, f32[5,16,128]{2,1,0:T(8,128)}, u32[]{:S(2)}) copy-start(f32[5,16,128]{2,1,0:T(8,128)} %copy-done.4) | copy-start | bytes 122884
  126.9 16.5 %copy-start.2 = (f32[32,5,16,128]{3,2,1,0:T(8,128)}, f32[32,5,16,128]{3,2,1,0:T(8,128)S(1)}, u32[]{:S(2)}) copy-start(f32[32,5,16,128]{3,2,1,0:T(8,128)S(1)} %constant_dynamic-update-slice_fusion) | copy-start | bytes 3932164
  178.2 111.8 %all-reduce.5.cloned.1.call-start = ((), (), s32[]{:S(2)}) async-start(), calls=%async_computation.1 | async-start | bytes 1048576 | tf_op jit(solution)/shard_map/psum | solution.py:129
  (9 other events, 13.0 us)
Sparse Core Ops, SparseCore 0:
  178.3 76.6 all-reduce.2
  257.5 32.4 all-reduce.4
